TPU v7x, 512 devices: a whole 4x4x16 slice. The times are simulated.
512 devices in a mesh: dp: 32 (over y_hi, z), expert: 16 (over y_lo, x, core).
Axes of the slice: x: 4, y: 4 (y_hi: 2, y_lo: 2; y = y_hi * 2 + y_lo), z: 16, core: 2. Of those that a mesh axis runs over, the one named last changes fastest.
Arguments:
- residual_in: bfloat16 [1536, 2048], P('dp', 'expert'), may hold values from -36 to 36
- attention_values: bfloat16 [1536, 2048], P('dp', 'expert'), may hold values from -6 to 6
- out_weight: bfloat16 [2048, 2048], P('expert', 'dp'), may hold values from -0.25 to 0.25
- norm_gain: float32 [2048], replicated, may hold values from 0.1 to 1.9
- shared_gate: bfloat16 [2816, 2048], P('expert'), may hold values from -0.125 to 0.125
- shared_up: bfloat16 [2816, 2048], P('expert'), may hold values from -0.125 to 0.125
- shared_down: bfloat16 [2816, 2048], P('expert'), may hold values from -0.15625 to 0.15625
- expert_gate: bfloat16 [64, 1408, 2048], P('dp', 'expert'), may hold values from -0.125 to 0.125
- expert_up: bfloat16 [64, 1408, 2048], P('dp', 'expert'), may hold values from -0.125 to 0.125
- expert_down: bfloat16 [64, 1408, 2048], P('dp', 'expert'), may hold values from -0.21875 to 0.21875
- expert_ids: int32 [1536, 6], P('dp'), may hold values from 0 to 63, all different within a row; in each aligned block of 48 rows (0 to 47, 48 to 95, ...) at most 10 rows name the same one
- gate_weights: float32 [1536, 6], P('dp'), may hold values from 0.02 to 0.5
Outputs:
- layer_out: bfloat16 [1536, 2048], P('dp', 'expert')
Inputs may be any that keep to these rules, and one draw needn't show every extreme that they name: `expert_ids`: each token names 6 different experts; among the 48 tokens of one index of dp (aligned blocks of rows) no expert is named by more than 10 tokens, a bound that some block reaches.
All inputs are finite; a program needn't handle non-finite values.
Results may differ from a plain program's by a relative error of at most 0.0035.
Values may be sent and summed in bfloat16 or wider, within the bound.
A program may use at most 128 MiB of HBM per device.

v0:
```python
import jax
import jax.numpy as jnp
from jax import lax
from jax.sharding import PartitionSpec as P

epsilon = 1e-06


def by_rows(left, right):
    return lax.dot_general(
        left, right, (((1,), (1,)), ((), ())), preferred_element_type=jnp.float32
    )


def expert_slots(expert_ids, experts, capacity):
    token_count, choose = expert_ids.shape
    flat_ids = expert_ids.reshape(-1)
    matches = (flat_ids[:, None] == jnp.arange(experts, dtype=jnp.int32)[None, :]).astype(jnp.int32)
    earlier = jnp.cumsum(matches, axis=0) - matches
    target = flat_ids * capacity + jnp.sum(earlier * matches, axis=1)
    return target.reshape(token_count, choose)


def collect_rows(returned_rows, slot_index, gate_weights):
    token_count, choose = slot_index.shape
    picked = returned_rows[slot_index.reshape(-1)].reshape(
        token_count, choose, returned_rows.shape[1]
    )
    return jnp.sum(picked * gate_weights[:, :, None], axis=1)


def expert_apply(buffer, expert_gate, expert_up, expert_down):
    gate_part = jnp.einsum(
        "slmd,lfd->slmf", buffer, expert_gate, preferred_element_type=jnp.float32
    )
    up_part = jnp.einsum("slmd,lfd->slmf", buffer, expert_up, preferred_element_type=jnp.float32)
    active = (jax.nn.silu(gate_part) * up_part).astype(jnp.bfloat16)
    return jnp.einsum("slmf,lfd->slmd", active, expert_down, preferred_element_type=jnp.float32)


def shards(
    residual_in,
    attention_values,
    out_weight,
    norm_gain,
    shared_gate,
    shared_up,
    shared_down,
    expert_gate,
    expert_up,
    expert_down,
    expert_ids,
    gate_weights,
):
    row_count = residual_in.shape[0]
    slice_width = residual_in.shape[1]
    expert_size = lax.axis_size("expert")
    batch_size = lax.axis_size("dp")
    full_width = slice_width * expert_size
    local_experts = expert_gate.shape[0]
    experts = local_experts * batch_size
    choose = expert_ids.shape[1]
    capacity = 2 * ((row_count * choose + experts - 1) // experts)
    column_start = lax.axis_index("expert") * slice_width
    head_terms = jnp.dot(
        attention_values,
        lax.all_gather(out_weight, "dp", axis=1, tiled=True),
        preferred_element_type=jnp.float32,
    )
    residual_own = residual_in.astype(jnp.float32)
    current = lax.dynamic_slice_in_dim(head_terms, column_start, slice_width, 1)
    head_terms = lax.dynamic_update_slice_in_dim(
        head_terms, current + residual_own, column_start, 1
    )
    residual = lax.psum(head_terms, "expert")
    inverse_rms = lax.rsqrt(jnp.mean(residual * residual, axis=1, keepdims=True) + epsilon)
    normed = (residual * inverse_rms * norm_gain).astype(jnp.bfloat16)
    residual_slice = lax.dynamic_slice_in_dim(residual, column_start, slice_width, 1)
    shared_active = (jax.nn.silu(by_rows(normed, shared_gate)) * by_rows(normed, shared_up)).astype(
        jnp.bfloat16
    )
    shared_terms = jnp.dot(shared_active, shared_down, preferred_element_type=jnp.float32)
    slot_index = expert_slots(expert_ids, experts, capacity)
    places = (
        slot_index[:, :, None] == jnp.arange(experts * capacity, dtype=jnp.int32)[None, None, :]
    )
    selector = jnp.any(places, axis=1).astype(jnp.bfloat16)
    slot_rows = lax.dot_general(
        selector, normed, (((0,), (0,)), ((), ())), preferred_element_type=jnp.float32
    )
    buffer = slot_rows.astype(jnp.bfloat16).reshape(batch_size, local_experts, capacity, full_width)
    partials = expert_apply(
        lax.all_to_all(buffer, "dp", split_axis=0, concat_axis=0, tiled=True),
        expert_gate,
        expert_up,
        expert_down,
    )
    returned = lax.all_to_all(partials, "dp", split_axis=0, concat_axis=0, tiled=True)
    routed_terms = collect_rows(
        returned.reshape(experts * capacity, full_width), slot_index, gate_weights
    )
    totals = lax.psum_scatter(
        shared_terms + routed_terms, "expert", scatter_dimension=1, tiled=True
    )
    return (residual_slice + totals).astype(jnp.bfloat16)


def solution(mesh):
    return jax.shard_map(
        shards,
        mesh=mesh,
        in_specs=(
            P("dp", "expert"),
            P("dp", "expert"),
            P("expert", "dp"),
            P(),
            P("expert", None),
            P("expert", None),
            P("expert", None),
            P("dp", "expert", None),
            P("dp", "expert", None),
            P("dp", "expert", None),
            P("dp", None),
            P("dp", None),
        ),
        out_specs=P("dp", "expert"),
        check_vma=False,
    )
```

profile of v0, /device:TPU:32, one launch (start us, length us, event | category | flops | bytes accessed | tf_op | source)
XLA Modules:
  0.0 723.8 jit_solution(14739102939381321039)
XLA Ops:
  6.5 0.0 copy-start
  6.5 0.0 copy-start.6
  6.5 0.0 all-reduce.3.cloned.1.call-start
  6.5 81.4 %all_gather.3 = bf16[128,2048]{0,1:T(8,128)(2,1)S(1)} all-gather(bf16[128,64]{0,1:T(8,128)(2,1)} %param.14), channel_id=1, replica_groups=mesh['dp'=32,'expert'=16] {'dp'}, dimensions={1}, use_global_device_ids=true | all-gather | bytes 540672 | tf_op jit(solution)/shard_map/all_gather | solution.py:67
  87.9 1.0 fusion.42
  88.9 0.7 add_dynamic-update-slice_fusion
  89.6 0.0 copy-start.1
  89.6 0.7 copy-done.1
  90.4 0.0 all-reduce.3.cloned.1.call-update
  90.4 0.8 copy.41
  91.2 0.1 eq.35
  91.4 0.9 reduce-window.6
  92.3 0.2 slice_reduce_fusion
  92.5 0.1 bitcast_bitcast_fusion
  92.7 0.1 reduce_sum.33
  92.8 0.6 broadcast_multiply_fusion
  93.4 0.1 copy.45
  93.5 0.8 fusion.19
  94.3 121.7 %all-reduce.3.cloned.1.call-done = f32[48,2048]{1,0:T(8,128)} async-done(((f32[48,2048]{1,0:T(8,128)}), f32[48,2048]{1,0:T(8,128)}) %all-reduce.3.cloned.1.call-update) | async-done | bytes 393232 | tf_op jit(solution)/shard_map/psum | solution.py:75
  216.0 1.1 multiply_reduce_fusion.1
  217.1 0.0 copy-done.6
  217.1 1.1 multiply_convert_fusion
  218.3 1.6 convolution_convert_fusion
  219.9 2.8 reshape.68
  222.7 4.9 copy.46
  227.6 0.0 copy-start.8
  227.6 138.5 %all_to_all.10 = bf16[32,2,10,2048]{3,1,2,0:T(2,128)(2,1)S(1)} all-to-all(bf16[32,2,10,2048]{3,1,2,0:T(2,128)(2,1)S(1)} %copy.46), channel_id=1, replica_groups=mesh['dp'=32,'expert'=16] {'dp'}, dimensions={0} | all-to-all | bytes 5242880 | tf_op jit(solution)/shard_map/all_to_all | solution.py:93
  366.1 0.0 copy-done.8
  366.1 2.3 fusion.4
  368.4 0.0 copy-done
  368.4 5.9 convolution_bitcast_fusion
  374.3 8.8 %copy.49 = f32[32,2,10,2048]{3,1,2,0:T(2,128)} copy(f32[32,2,10,2048]{3,0,2,1:T(8,128)} %convolution_bitcast_fusion) | data formatting | bytes 10485760 | tf_op jit(solution)/shard_map/slmf,lfd->slmd/transpose | solution.py:38
  383.1 0.0 copy-start.5
  383.1 0.0 copy-start.7
  383.1 0.0 copy-start.4
  383.1 4.8 all-to-all-start.1
  387.9 0.3 reduce-scatter.2.cloned.1.call-start
  388.2 0.0 copy-done.5
  388.2 0.1 mul.78
  388.3 0.0 copy-done.7
  388.4 0.1 copy.51
  388.5 0.0 copy-done.4
  388.5 0.3 fusion.43
  388.8 234.1 %all-to-all-done.1 = f32[32,2,10,2048]{3,1,2,0:T(2,128)} async-done(((f32[32,2,10,2048]{3,1,2,0:T(2,128)}), f32[32,2,10,2048]{3,1,2,0:T(2,128)}, u32[]{:S(2)}, u32[]{:S(2)}) %all-to-all-start.1) | async-done | bytes 5242912 | tf_op jit(solution)/shard_map/all_to_all | solution.py:98
  623.0 10.3 %copy.50 = f32[32,2,10,2048]{3,2,1,0:T(8,128)} copy(f32[32,2,10,2048]{3,1,2,0:T(2,128)} %all-to-all-done.1) | data formatting | bytes 10485760 | tf_op jit(solution)/shard_map/all_to_all | solution.py:98
  633.3 7.4 %reshape.69 = f32[640,2048]{1,0:T(8,128)} reshape(f32[32,2,10,2048]{3,2,1,0:T(8,128)} %copy.50) | data formatting | bytes 10485760 | tf_op jit(solution)/shard_map/reshape | solution.py:100
  640.7 6.8 gather_fusion
  647.4 1.8 reshape.70
  649.3 0.0 copy-start.2
  649.3 0.0 copy-start.3
  649.3 3.1 multiply_reduce_fusion
  652.4 0.0 copy-done.2
  652.4 0.0 copy-done.3
  652.5 1.4 convolution_add_fusion
  653.9 0.0 reduce-scatter.2.cloned.1.call-update
  653.9 61.7 %reduce-scatter.2.cloned.1.call-done = f32[48,128]{1,0:T(8,128)} async-done(((f32[48,2048]{1,0:T(8,128)}), f32[48,128]{1,0:T(8,128)}) %reduce-scatter.2.cloned.1.call-update) | async-done | bytes 24592 | tf_op jit(solution)/shard_map/reduce_scatter | solution.py:102
  715.6 1.4 add_convert_fusion
  (7 shorter events, 0.1 us)
Async XLA Ops:
  6.5 361.9 %copy-start = (bf16[2,88,2048]{2,1,0:T(8,128)(2,1)S(1)}, bf16[2,88,2048]{2,1,0:T(8,128)(2,1)}, u32[]{:S(2)}) copy-start(bf16[2,88,2048]{2,1,0:T(8,128)(2,1)} %param.21) | copy-start | bytes 2162692
  6.5 210.6 %copy-start.6 = (f32[2048]{0:T(1024)S(1)}, f32[2048]{0:T(1024)}, u32[]{:S(2)}) copy-start(f32[2048]{0:T(1024)} %param.15) | copy-start | bytes 24580
  6.5 209.5 %all-reduce.3.cloned.1.call-start = ((), (), s32[]{:S(2)}) async-start(), calls=%async_computation.3 | async-start | bytes 786432 | tf_op jit(solution)/shard_map/psum | solution.py:75
  89.6 0.7 copy-start.1
  227.6 138.5 %copy-start.8 = (bf16[2,88,2048]{2,1,0:T(8,128)(2,1)S(1)}, bf16[2,88,2048]{2,1,0:T(8,128)(2,1)}, u32[]{:S(2)}) copy-start(bf16[2,88,2048]{2,1,0:T(8,128)(2,1)} %param.19) | copy-start | bytes 2162692
  383.1 5.1 copy-start.5
  383.1 5.2 copy-start.7
  383.1 5.4 copy-start.4
  383.1 239.9 %all-to-all-start.1 = ((f32[32,2,10,2048]{3,1,2,0:T(2,128)}), f32[32,2,10,2048]{3,1,2,0:T(2,128)}, u32[]{:S(2)}, u32[]{:S(2)}) async-start(f32[32,2,10,2048]{3,1,2,0:T(2,128)} %copy.49), calls=%async_computation.1 | async-start | bytes 10485760 | tf_op jit(solution)/shard_map/all_to_all | solution.py:98
  387.9 327.7 %reduce-scatter.2.cloned.1.call-start = ((), (), s32[]{:S(2)}) async-start(), calls=%async_computation.4 | async-start | bytes 417792 | tf_op jit(solution)/shard_map/reduce_scatter | solution.py:102
  649.3 3.1 copy-start.2
  649.3 3.2 copy-start.3
Sparse Core Ops, SparseCore 0:
  90.5 125.4 all-reduce.2
  654.0 61.5 reduce-scatter.1
where the time goes:
time: 725 us; the launch traced here: 724 us
  waiting for transfers between devices  418 us (58%)
  blocking collectives  220 us (30%)
  local copies, waits for them, and re-layouts  45.1 us (6%)
  between operations  13.6 us (2%)
  matrix products  12.6 us (2%)
  other arithmetic  9.98 us (1%)
    all_to_all x1, waiting for transfers between devices, shards(): lax.all_to_all(partials, 'dp', split_axis=0, concat_axis=0, tiled=True)  234 us
    all_to_all x1, blocking collectives, shards(): lax.all_to_all(buffer, 'dp', split_axis=0, concat_axis=0, tiled=True)  138 us
    psum x1, waiting for transfers between devices, shards(): residual = lax.psum(head_terms, 'expert')  122 us
    all_gather x1, blocking collectives, shards(): lax.all_gather(out_weight, 'dp', axis=1, tiled=True)  81.4 us
    reduce_scatter x1, waiting for transfers between devices, shards(): lax.psum_scatter(shared_terms + routed_terms, 'expert', scatter_dimension...  61.7 us
  transfers between devices with their start and end apart: 3, of which 3 were waited for; matrix products, arithmetic and copies ran while one was open for 1% of the time, Pallas kernels for 0%

commit v1 on v0

--- a/solution.py
+++ b/solution.py
@@ -4,6 +4,11 @@
 from jax.sharding import PartitionSpec as P
 
 epsilon = 1e-06
+
+
+def gather_and_add(x, axis):
+    parts = lax.all_gather(x, axis)
+    return jnp.sum(parts, axis=0)
 
 
 def by_rows(left, right):
@@ -72,7 +77,7 @@
     head_terms = lax.dynamic_update_slice_in_dim(
         head_terms, current + residual_own, column_start, 1
     )
-    residual = lax.psum(head_terms, "expert")
+    residual = gather_and_add(head_terms, "expert")
     inverse_rms = lax.rsqrt(jnp.mean(residual * residual, axis=1, keepdims=True) + epsilon)
     normed = (residual * inverse_rms * norm_gain).astype(jnp.bfloat16)
     residual_slice = lax.dynamic_slice_in_dim(residual, column_start, slice_width, 1)

time: 725 us -> 642 us (0.89)
  waiting for transfers between devices: 418 us -> 333 us
    psum x1 -> x0, waiting for transfers between devices: 122 us -> none  [shards(): residual = lax.psum(head_terms, 'expert')]
    all_gather x0 -> x1, waiting for transfers between devices: none -> 39.9 us  [gather_and_add(): parts = lax.all_gather(x, axis)]
where the time goes in v1:
time: 642 us; the launch traced here: 641 us
  waiting for transfers between devices  333 us (52%)
  blocking collectives  220 us (34%)
  local copies, waits for them, and re-layouts  45.1 us (7%)
  between operations  13.6 us (2%)
  matrix products  12.6 us (2%)
  other arithmetic  11.1 us (2%)
    all_to_all x1, waiting for transfers between devices, shards(): lax.all_to_all(partials, 'dp', split_axis=0, concat_axis=0, tiled=True)  234 us
    all_to_all x1, blocking collectives, shards(): lax.all_to_all(buffer, 'dp', split_axis=0, concat_axis=0, tiled=True)  139 us
    all_gather x1, blocking collectives, shards(): lax.all_gather(out_weight, 'dp', axis=1, tiled=True)  81.4 us
    reduce_scatter x1, waiting for transfers between devices, shards(): lax.psum_scatter(shared_terms + routed_terms, 'expert', scatter_dimension...  59.4 us
    all_gather x1, waiting for transfers between devices, gather_and_add(): parts = lax.all_gather(x, axis)  39.9 us
  transfers between devices with their start and end apart: 3, of which 3 were waited for; matrix products, arithmetic and copies ran while one was open for 1% of the time, Pallas kernels for 0%

profile of v1, /device:TPU:32, one launch (start us, length us, event | category | flops | bytes accessed | tf_op | source)
XLA Modules:
  0.0 641.1 jit_solution(18441331510742704819)
XLA Ops:
  6.5 0.0 copy-start
  6.5 0.0 copy-start.8
  6.5 0.0 all-gather.2.cloned.1.call-start
  6.5 81.4 %all_gather.11 = bf16[128,2048]{0,1:T(8,128)(2,1)S(1)} all-gather(bf16[128,64]{0,1:T(8,128)(2,1)} %param.14), channel_id=1, replica_groups=mesh['dp'=32,'expert'=16] {'dp'}, dimensions={1}, use_global_device_ids=true | all-gather | bytes 540672 | tf_op jit(solution)/shard_map/all_gather | solution.py:72
  87.9 1.0 fusion.42
  89.0 0.7 bitcast_dynamic-update-slice_fusion
  89.7 0.0 copy-start.2
  89.7 0.8 copy-done.2
  90.5 0.0 all-gather.2.cloned.1.call-update
  90.5 0.0 copy-done.8
  90.5 0.1 copy.41
  90.6 0.1 eq.35
  90.8 0.9 reduce-window.6
  91.7 0.2 slice_reduce_fusion
  91.9 0.1 bitcast_bitcast_fusion
  92.1 0.1 reduce_sum.43
  92.2 0.6 broadcast_multiply_fusion
  92.8 0.1 copy.45
  92.9 0.8 fusion.19
  93.7 0.0 copy-start.7
  93.7 39.9 %all-gather.2.cloned.1.call-done = f32[16,48,2048]{2,1,0:T(8,128)} async-done(((f32[1,48,2048]{2,1,0:T(8,128)}), f32[16,48,2048]{2,1,0:T(8,128)}) %all-gather.2.cloned.1.call-update) | async-done | bytes 6291472 | tf_op jit(solution)/shard_map/all_gather | solution.py:10
  133.6 3.1 reduce_sum.40
  136.8 0.0 copy-start.1
  136.8 0.1 multiply_reduce_fusion.1
  136.9 0.6 copy-done.1
  137.5 0.0 copy-done.7
  137.5 0.1 multiply_convert_fusion
  137.6 1.6 convolution_convert_fusion
  139.3 2.8 reshape.70
  142.0 4.9 copy.46
  147.0 0.0 copy-start.10
  147.0 139.1 %all_to_all.10 = bf16[32,2,10,2048]{3,1,2,0:T(2,128)(2,1)S(1)} all-to-all(bf16[32,2,10,2048]{3,1,2,0:T(2,128)(2,1)S(1)} %copy.46), channel_id=1, replica_groups=mesh['dp'=32,'expert'=16] {'dp'}, dimensions={0} | all-to-all | bytes 5242880 | tf_op jit(solution)/shard_map/all_to_all | solution.py:98
  286.1 0.0 copy-done.10
  286.1 2.3 fusion.4
  288.4 0.0 copy-done
  288.4 5.9 convolution_bitcast_fusion
  294.3 8.8 %copy.49 = f32[32,2,10,2048]{3,1,2,0:T(2,128)} copy(f32[32,2,10,2048]{3,0,2,1:T(8,128)} %convolution_bitcast_fusion) | data formatting | bytes 10485760 | tf_op jit(solution)/shard_map/slmf,lfd->slmd/transpose | solution.py:43
  303.1 0.0 copy-start.6
  303.1 0.0 copy-start.9
  303.1 0.0 copy-start.5
  303.1 4.8 all-to-all-start.1
  307.9 0.3 reduce-scatter.2.cloned.1.call-start
  308.2 0.0 copy-done.6
  308.2 0.1 mul.78
  308.3 0.0 copy-done.9
  308.3 0.1 copy.51
  308.5 0.0 copy-done.5
  308.5 0.3 fusion.43
  308.8 233.7 %all-to-all-done.1 = f32[32,2,10,2048]{3,1,2,0:T(2,128)} async-done(((f32[32,2,10,2048]{3,1,2,0:T(2,128)}), f32[32,2,10,2048]{3,1,2,0:T(2,128)}, u32[]{:S(2)}, u32[]{:S(2)}) %all-to-all-start.1) | async-done | bytes 5242912 | tf_op jit(solution)/shard_map/all_to_all | solution.py:103
  542.6 10.3 %copy.50 = f32[32,2,10,2048]{3,2,1,0:T(8,128)} copy(f32[32,2,10,2048]{3,1,2,0:T(2,128)} %all-to-all-done.1) | data formatting | bytes 10485760 | tf_op jit(solution)/shard_map/all_to_all | solution.py:103
  552.9 7.4 %reshape.71 = f32[640,2048]{1,0:T(8,128)} reshape(f32[32,2,10,2048]{3,2,1,0:T(8,128)} %copy.50) | data formatting | bytes 10485760 | tf_op jit(solution)/shard_map/reshape | solution.py:105
  560.3 6.8 %gather_fusion = f32[288,2048]{1,0:T(8,128)S(1)} fusion(f32[640,2048]{1,0:T(8,128)} %reshape.71, s32[1024]{0:T(1024)S(1)} %pad_clamp_fusion), kind=kCustom, calls=%fused_computation | custom fusion | bytes 4719744 | tf_op jit(solution)/shard_map/gather | solution.py:31
  567.1 1.8 reshape.72
  568.9 0.0 copy-start.3
  568.9 0.0 copy-start.4
  568.9 3.1 multiply_reduce_fusion
  572.0 0.0 copy-done.3
  572.0 0.0 copy-done.4
  572.1 1.4 convolution_add_fusion
  573.5 0.0 reduce-scatter.2.cloned.1.call-update
  573.5 59.4 %reduce-scatter.2.cloned.1.call-done = f32[48,128]{1,0:T(8,128)} async-done(((f32[48,2048]{1,0:T(8,128)}), f32[48,128]{1,0:T(8,128)}) %reduce-scatter.2.cloned.1.call-update) | async-done | bytes 24592 | tf_op jit(solution)/shard_map/reduce_scatter | solution.py:107
  632.9 1.4 add_convert_fusion
  (8 shorter events, 0.2 us)
Async XLA Ops:
  6.5 281.9 %copy-start = (bf16[2,88,2048]{2,1,0:T(8,128)(2,1)S(1)}, bf16[2,88,2048]{2,1,0:T(8,128)(2,1)}, u32[]{:S(2)}) copy-start(bf16[2,88,2048]{2,1,0:T(8,128)(2,1)} %param.21) | copy-start | bytes 2162692
  6.5 83.9 %copy-start.8 = (s32[48,6]{0,1:T(8,128)S(1)}, s32[48,6]{0,1:T(8,128)}, u32[]{:S(2)}) copy-start(s32[48,6]{0,1:T(8,128)} %param.22) | copy-start | bytes 3460
  6.5 127.1 %all-gather.2.cloned.1.call-start = ((), (), s32[]{:S(2)}) async-start(), calls=%async_computation.3 | async-start | bytes 6684672 | tf_op jit(solution)/shard_map/all_gather | solution.py:10
  89.7 0.8 copy-start.2
  93.7 43.8 %copy-start.7 = (f32[2048]{0:T(1024)S(1)}, f32[2048]{0:T(1024)}, u32[]{:S(2)}) copy-start(f32[2048]{0:T(1024)} %param.15) | copy-start | bytes 24580
  136.8 0.7 copy-start.1
  147.0 139.1 %copy-start.10 = (bf16[2,88,2048]{2,1,0:T(8,128)(2,1)S(1)}, bf16[2,88,2048]{2,1,0:T(8,128)(2,1)}, u32[]{:S(2)}) copy-start(bf16[2,88,2048]{2,1,0:T(8,128)(2,1)} %param.19) | copy-start | bytes 2162692
  303.1 5.1 copy-start.6
  303.1 5.2 copy-start.9
  303.1 5.4 copy-start.5
  303.1 239.5 %all-to-all-start.1 = ((f32[32,2,10,2048]{3,1,2,0:T(2,128)}), f32[32,2,10,2048]{3,1,2,0:T(2,128)}, u32[]{:S(2)}, u32[]{:S(2)}) async-start(f32[32,2,10,2048]{3,1,2,0:T(2,128)} %copy.49), calls=%async_computation.1 | async-start | bytes 10485760 | tf_op jit(solution)/shard_map/all_to_all | solution.py:103
  307.9 325.0 %reduce-scatter.2.cloned.1.call-start = ((), (), s32[]{:S(2)}) async-start(), calls=%async_computation.4 | async-start | bytes 417792 | tf_op jit(solution)/shard_map/reduce_scatter | solution.py:107
  568.9 3.1 copy-start.3
  568.9 3.2 copy-start.4
Sparse Core Ops, SparseCore 0:
  90.6 42.9 all-gather.1
  573.6 59.2 reduce-scatter.1
